TPU v7x, 32 devices: a whole 2x2x4 slice. The times are simulated.
32 devices in a mesh: gx: 8 (over z, x), gy: 4 (over y, core).
Axes of the slice: x: 2, y: 2, z: 4, core: 2. Of those that a mesh axis runs over, the one named last changes fastest.
Arguments:
- source_snaps: float32 [4, 384, 64, 256], P(None, 'gx', 'gy'), may hold values from -6 to 6
- receiver_snaps: float32 [4, 384, 64, 256], P(None, 'gx', 'gy'), may hold values from -6 to 6
- snap_pairs: int32 [3, 2], replicated, may hold values from 0 to 3
- offset_lags: int32 [17], replicated, may hold values from -24 to 24, as said below
- weight_table: float32 [4, 17], replicated, may hold values from 0.2 to 1
- weight_index: int32 [3], replicated, may hold values from 0 to 3
Outputs:
- adjoint_source: float32 [3, 384, 64, 256], P(None, 'gx', 'gy')
- adjoint_receiver: float32 [3, 384, 64, 256], P(None, 'gx', 'gy')
Inputs may be any that keep to these rules, and one draw needn't show every extreme that they name: `offset_lags`: strictly increasing; the first entry is -24 and the last is 24.
All inputs are finite; a program needn't handle non-finite values.
Results may differ from a plain program's by a relative error of at most 0.00002.
Values sent between devices are 32-bit elements; how exact they have to be, the bound alone decides.
A program may use at most 128 MiB of HBM per device.

v0:
```python
import jax
import jax.numpy as jnp
from jax import lax
from jax.sharding import PartitionSpec as P

NOFF = 17
MAXLAG = 24


def with_halo(block, sides, width):
    for axis, dim in sides:
        count = lax.axis_size(axis)
        forward = [(i, i + 1) for i in range(count - 1)]
        backward = [(target, source) for source, target in forward]
        low = lax.ppermute(
            lax.slice_in_dim(block, block.shape[dim] - width, None, axis=dim), axis, forward
        )
        high = lax.ppermute(lax.slice_in_dim(block, 0, width, axis=dim), axis, backward)
        block = jnp.concatenate([low, block, high], axis=dim)
    return block


def passed_along(block, axis, distance):
    devices = range(lax.axis_size(axis))
    route = [(i - distance, i) for i in devices if i - distance in devices]
    return lax.ppermute(block, axis, route)


def smooth_pairs(values):
    return (
        values[:, :, :-4]
        + values[:, :, 4:]
        + 4.0 * (values[:, :, 1:-3] + values[:, :, 3:-1])
        + 6.0 * values[:, :, 2:-2]
    ) / 16.0


def place_add(totals, values, start):
    current = lax.dynamic_slice_in_dim(totals, start, values.shape[1], 1)
    return lax.dynamic_update_slice_in_dim(totals, current + values, start, 1)


def local(source_snaps, receiver_snaps, snap_pairs, offset_lags, weight_table, weight_index):
    cells_x = source_snaps.shape[1]
    cells_y = source_snaps.shape[2]
    depth = source_snaps.shape[3]
    pair_count = snap_pairs.shape[0]
    chosen = [source_snaps[snap_pairs[pair_index, 0]] for pair_index in range(pair_count)]
    chosen = chosen + [
        receiver_snaps[snap_pairs[pair_index, 1]] for pair_index in range(pair_count)
    ]
    fields = jnp.stack(chosen)
    widened = with_halo(fields, (("gy", 2),), 2)
    pair_weights = weight_table[weight_index]
    extended = with_halo(widened, (("gx", 1),), MAXLAG)
    source_wide = extended[:pair_count]
    receiver_wide = extended[pair_count:]

    def step(offset, running):
        source_total, receiver_total = running
        offset_lag = offset_lags[offset]
        weight = pair_weights[:, offset][:, None, None, None]
        shifted_source = lax.dynamic_slice_in_dim(source_wide, MAXLAG - offset_lag, cells_x, 1)
        shifted_receiver = lax.dynamic_slice_in_dim(receiver_wide, MAXLAG + offset_lag, cells_x, 1)
        smoothed = smooth_pairs(weight * shifted_source * shifted_receiver)
        source_total = place_add(
            source_total, smoothed * shifted_receiver[:, :, 2:-2], MAXLAG - offset_lag
        )
        receiver_total = place_add(
            receiver_total, smoothed * shifted_source[:, :, 2:-2], MAXLAG + offset_lag
        )
        return (source_total, receiver_total)

    zeros = jnp.zeros((pair_count, cells_x + 2 * MAXLAG, cells_y, depth), jnp.float32)
    source_total, receiver_total = lax.fori_loop(0, NOFF, step, (zeros, zeros))
    totals = jnp.concatenate([source_total, receiver_total], axis=0)
    from_above = passed_along(totals[:, :MAXLAG], "gx", -1)
    from_below = passed_along(totals[:, cells_x + MAXLAG :], "gx", 1)
    owned = totals[:, MAXLAG : cells_x + MAXLAG]
    owned = owned.at[:, :MAXLAG].add(from_below)
    owned = owned.at[:, cells_x - MAXLAG :].add(from_above)
    return (owned[:pair_count], owned[pair_count:])


def solution(mesh):
    return jax.shard_map(
        local,
        mesh=mesh,
        in_specs=(P(None, "gx", "gy", None), P(None, "gx", "gy", None), P(), P(), P(), P()),
        out_specs=(P(None, "gx", "gy", None), P(None, "gx", "gy", None)),
        check_vma=False,
    )
```

profile of v0, /device:TPU:6, one launch (start us, length us, event | category | flops | bytes accessed | tf_op | source)
XLA Modules:
  0.0 588.4 jit_solution(8481897765342315444)
XLA Ops:
  25.4 3.6 collective-permute-start.1
  29.0 5.6 collective-permute-done
  37.2 3.2 fusion.15
  40.4 3.4 collective-permute-start.2
  43.9 2.8 collective-permute-start.3
  48.6 115.9 %collective-permute-done.2 = f32[6,24,20,256]{3,1,2,0:T(8,128)S(1)} collective-permute-done((f32[6,24,20,256]{3,1,2,0:T(8,128)}, f32[6,24,20,256]{3,1,2,0:T(8,128)S(1)}, u32[]{:S(2)}, u32[]{:S(2)}) %collective-permute-start.2) | collective-permute-done | bytes 2949152 | tf_op jit(solution)/shard_map/ppermute | solution.py:15
  164.5 8.6 %pad_maximum_fusion = f32[6,96,20,256]{3,1,2,0:T(8,128)} fusion(f32[6,24,20,256]{3,1,2,0:T(8,128)} %collective-permute-done.3, f32[6,48,2,256]{3,1,2,0:T(8,128)} %copy-done.7, f32[6,48,16,256]{3,1,2,0:T(8,128)} %copy-done.6, f32[6,48,2,256]{3,1,2,0:T(8,128)S(1)} %collective-permute-done, f32[6,24,20,256]{3,1,2,0:T(8,128)S(1)} %collective-permute-done.2), kind=kLoop, calls=%fused_computation.19 | loop fusion | flops 11796480 | bytes 23592960 | tf_op jit(solution)/shard_map/concatenate | solution.py:19
  173.1 10.2 %fusion.13 = (f32[3,96,20,256]{3,1,2,0:T(8,128)}, f32[3,96,20,256]{3,1,2,0:T(8,128)}) fusion(f32[6,96,20,256]{3,1,2,0:T(8,128)} %pad_maximum_fusion), kind=kLoop, calls=%fused_computation.42 | loop fusion | bytes 23592960 | tf_op jit(solution)/shard_map/slice | solution.py:57
  183.3 2.8 broadcast_in_dim.6.clone
  188.8 288.6 %while.20 = (s32[]{:T(128)}, f32[3,96,16,256]{3,2,1,0:T(8,128)}, f32[3,96,16,256]{3,2,1,0:T(8,128)}, s32[17]{0:T(128)S(1)}, f32[3,17]{0,1:T(8,128)S(1)}, /*index...) while((s32[]{:T(128)}, f32[3,96,16,256]{3,2,1,0:T(8,128)}, ...), condition=%wide.region_1.0_spmd, body=%wide.region_0.0_spmd.sunk | while | flops 7962634 | bytes 123273640 | solution.py:75
  192.0 4.0 constant_dynamic-slice_fusion.10
  196.0 3.6 fusion.24
  208.9 4.1 constant_dynamic-slice_fusion.10
  213.0 3.6 fusion.24
  225.9 4.1 constant_dynamic-slice_fusion.10
  230.0 3.6 fusion.24
  242.9 4.1 constant_dynamic-slice_fusion.10
  247.0 3.6 fusion.24
  259.8 4.1 constant_dynamic-slice_fusion.10
  264.0 3.6 fusion.24
  276.8 4.1 constant_dynamic-slice_fusion.10
  281.0 3.6 fusion.24
  293.8 4.1 constant_dynamic-slice_fusion.10
  298.0 3.6 fusion.24
  310.8 4.1 constant_dynamic-slice_fusion.10
  315.0 3.6 fusion.24
  327.8 4.1 constant_dynamic-slice_fusion.10
  332.0 3.6 fusion.24
  344.8 4.1 constant_dynamic-slice_fusion.10
  349.0 3.6 fusion.24
  361.8 4.1 constant_dynamic-slice_fusion.10
  366.0 3.6 fusion.24
  378.8 4.1 constant_dynamic-slice_fusion.10
  383.0 3.6 fusion.24
  395.8 4.1 constant_dynamic-slice_fusion.10
  400.0 3.6 fusion.24
  412.8 4.1 constant_dynamic-slice_fusion.10
  417.0 3.6 fusion.24
  429.8 4.1 constant_dynamic-slice_fusion.10
  434.0 3.6 fusion.24
  446.8 4.1 constant_dynamic-slice_fusion.10
  451.0 3.6 fusion.24
  463.8 4.0 constant_dynamic-slice_fusion.10
  467.8 3.6 fusion.24
  477.4 3.0 constant_dynamic-update-slice_fusion.1
  482.5 4.5 collective-permute-start.4
  489.9 94.2 %collective-permute-done.4 = f32[6,24,16,256]{3,2,1,0:T(8,128)S(1)} collective-permute-done((f32[6,24,16,256]{3,2,1,0:T(8,128)S(1)}, f32[6,24,16,256]{3,2,1,0:T(8,128)S(1)}, u32[]{:S(2)}, u32[]{:S(2)}) %collective-permute-start.4) | collective-permute-done | bytes 2359328 | tf_op jit(solution)/shard_map/ppermute | solution.py:26
  585.3 3.2 fusion.16
  (350 shorter events, 137.5 us)
Async XLA Ops:
  0.6 46.0 %copy-start = (f32[4,17]{1,0:T(4,128)S(1)}, f32[4,17]{1,0:T(4,128)}, u32[]{:S(2)}) copy-start(f32[4,17]{1,0:T(4,128)} %param.16) | copy-start | bytes 820
  23.3 13.8 %copy-start.6 = (f32[6,48,16,256]{3,1,2,0:T(8,128)}, f32[6,48,16,256]{3,1,2,0:T(8,128)S(1)}, u32[]{:S(2)}) copy-start(f32[6,48,16,256]{3,1,2,0:T(8,128)S(1)} %copy_dynamic-update-slice_fusion) | copy-start | bytes 14155780
  23.5 11.2 %collective-permute-start = (f32[6,48,2,256]{3,1,2,0:T(8,128)S(1)}, f32[6,48,2,256]{3,1,2,0:T(8,128)S(1)}, u32[]{:S(2)}, u32[]{:S(2)}) collective-permute-start(f32[6,48,2,256]{3,1,2,0:T(8,128)S(1)} %get-tuple-element.268), channel_id=1, source_target_pairs={{0,1},{1,2},{2,3},{4,5},{5,6},{6,7},{8,9},{9,10},{10,11},{12,13},{... | collective-permute-start | bytes 1769480 | tf_op jit(solution)/shard_map/ppermute | solution.py:15
  25.4 11.0 %collective-permute-start.1 = (f32[6,48,2,256]{3,1,2,0:T(8,128)S(1)}, f32[6,48,2,256]{3,1,2,0:T(8,128)S(1)}, u32[]{:S(2)}, u32[]{:S(2)}) collective-permute-start(f32[6,48,2,256]{3,1,2,0:T(8,128)S(1)} %get-tuple-element.269), channel_id=1, source_target_pairs={{1,0},{2,1},{3,2},{5,4},{6,5},{7,6},{9,8},{10,9},{11,10},{13,12},{... | collective-permute-start | bytes 1769480 | tf_op jit(solution)/shard_map/ppermute | solution.py:18
  37.2 9.4 %copy-start.9 = (s32[3]{0:T(128)S(1)}, s32[3]{0:T(128)}, u32[]{:S(2)}) copy-start(s32[3]{0:T(128)} %param.17) | copy-start | bytes 40
  40.4 124.1 %collective-permute-start.2 = (f32[6,24,20,256]{3,1,2,0:T(8,128)}, f32[6,24,20,256]{3,1,2,0:T(8,128)S(1)}, u32[]{:S(2)}, u32[]{:S(2)}) collective-permute-start(f32[6,24,20,256]{3,1,2,0:T(8,128)} %get-tuple-element.264), channel_id=1, source_target_pairs={{0,4},{4,8},{8,12},{12,16},{16,20},{20,24},{24,28},{1,5},{5,9},{9,... | collective-permute-start | bytes 8847368 | tf_op jit(solution)/shard_map/ppermute | solution.py:15
  43.9 120.6 %collective-permute-start.3 = (f32[6,24,20,256]{3,1,2,0:T(8,128)}, f32[6,24,20,256]{3,1,2,0:T(8,128)}, u32[]{:S(2)}, u32[]{:S(2)}) collective-permute-start(f32[6,24,20,256]{3,1,2,0:T(8,128)} %get-tuple-element.265), channel_id=1, source_target_pairs={{4,0},{8,4},{12,8},{16,12},{20,16},{24,20},{28,24},{5,1},{9,5},{13... | collective-permute-start | bytes 8847368 | tf_op jit(solution)/shard_map/ppermute | solution.py:18
  183.3 5.5 copy-start.10
  192.0 7.7 %slice-start = ((s8[4718592]{0:T(1024)(128)(4,1)}), s8[4194304]{0:T(1024)(128)(4,1)S(1)}, s32[]{:S(2)}) async-start(s8[4718592]{0:T(1024)(128)(4,1)} %bitcast.22), calls=%async_computation | async-start | bytes 8388608 | tf_op jit(solution)/shard_map/while
  196.0 3.7 slice-start.1
  196.0 5.3 slice-start.2
  208.8 7.8 %slice-start = ((s8[4718592]{0:T(1024)(128)(4,1)}), s8[4194304]{0:T(1024)(128)(4,1)S(1)}, s32[]{:S(2)}) async-start(s8[4718592]{0:T(1024)(128)(4,1)} %bitcast.22), calls=%async_computation | async-start | bytes 8388608 | tf_op jit(solution)/shard_map/while
  213.0 3.7 slice-start.1
  213.0 5.3 slice-start.2
  225.8 7.8 %slice-start = ((s8[4718592]{0:T(1024)(128)(4,1)}), s8[4194304]{0:T(1024)(128)(4,1)S(1)}, s32[]{:S(2)}) async-start(s8[4718592]{0:T(1024)(128)(4,1)} %bitcast.22), calls=%async_computation | async-start | bytes 8388608 | tf_op jit(solution)/shard_map/while
  230.0 5.3 slice-start.2
  242.8 7.8 %slice-start = ((s8[4718592]{0:T(1024)(128)(4,1)}), s8[4194304]{0:T(1024)(128)(4,1)S(1)}, s32[]{:S(2)}) async-start(s8[4718592]{0:T(1024)(128)(4,1)} %bitcast.22), calls=%async_computation | async-start | bytes 8388608 | tf_op jit(solution)/shard_map/while
  247.0 5.3 slice-start.2
  259.8 7.8 %slice-start = ((s8[4718592]{0:T(1024)(128)(4,1)}), s8[4194304]{0:T(1024)(128)(4,1)S(1)}, s32[]{:S(2)}) async-start(s8[4718592]{0:T(1024)(128)(4,1)} %bitcast.22), calls=%async_computation | async-start | bytes 8388608 | tf_op jit(solution)/shard_map/while
  264.0 5.3 slice-start.2
  276.8 7.8 %slice-start = ((s8[4718592]{0:T(1024)(128)(4,1)}), s8[4194304]{0:T(1024)(128)(4,1)S(1)}, s32[]{:S(2)}) async-start(s8[4718592]{0:T(1024)(128)(4,1)} %bitcast.22), calls=%async_computation | async-start | bytes 8388608 | tf_op jit(solution)/shard_map/while
  281.0 5.3 slice-start.2
  293.8 7.8 %slice-start = ((s8[4718592]{0:T(1024)(128)(4,1)}), s8[4194304]{0:T(1024)(128)(4,1)S(1)}, s32[]{:S(2)}) async-start(s8[4718592]{0:T(1024)(128)(4,1)} %bitcast.22), calls=%async_computation | async-start | bytes 8388608 | tf_op jit(solution)/shard_map/while
  298.0 5.3 slice-start.2
  310.8 7.8 %slice-start = ((s8[4718592]{0:T(1024)(128)(4,1)}), s8[4194304]{0:T(1024)(128)(4,1)S(1)}, s32[]{:S(2)}) async-start(s8[4718592]{0:T(1024)(128)(4,1)} %bitcast.22), calls=%async_computation | async-start | bytes 8388608 | tf_op jit(solution)/shard_map/while
  315.0 5.3 slice-start.2
  327.8 7.8 %slice-start = ((s8[4718592]{0:T(1024)(128)(4,1)}), s8[4194304]{0:T(1024)(128)(4,1)S(1)}, s32[]{:S(2)}) async-start(s8[4718592]{0:T(1024)(128)(4,1)} %bitcast.22), calls=%async_computation | async-start | bytes 8388608 | tf_op jit(solution)/shard_map/while
  332.0 5.3 slice-start.2
  344.8 7.8 %slice-start = ((s8[4718592]{0:T(1024)(128)(4,1)}), s8[4194304]{0:T(1024)(128)(4,1)S(1)}, s32[]{:S(2)}) async-start(s8[4718592]{0:T(1024)(128)(4,1)} %bitcast.22), calls=%async_computation | async-start | bytes 8388608 | tf_op jit(solution)/shard_map/while
  349.0 5.3 slice-start.2
  361.8 7.8 %slice-start = ((s8[4718592]{0:T(1024)(128)(4,1)}), s8[4194304]{0:T(1024)(128)(4,1)S(1)}, s32[]{:S(2)}) async-start(s8[4718592]{0:T(1024)(128)(4,1)} %bitcast.22), calls=%async_computation | async-start | bytes 8388608 | tf_op jit(solution)/shard_map/while
  366.0 5.3 slice-start.2
  378.8 7.8 %slice-start = ((s8[4718592]{0:T(1024)(128)(4,1)}), s8[4194304]{0:T(1024)(128)(4,1)S(1)}, s32[]{:S(2)}) async-start(s8[4718592]{0:T(1024)(128)(4,1)} %bitcast.22), calls=%async_computation | async-start | bytes 8388608 | tf_op jit(solution)/shard_map/while
  383.0 5.3 slice-start.2
  395.8 7.8 %slice-start = ((s8[4718592]{0:T(1024)(128)(4,1)}), s8[4194304]{0:T(1024)(128)(4,1)S(1)}, s32[]{:S(2)}) async-start(s8[4718592]{0:T(1024)(128)(4,1)} %bitcast.22), calls=%async_computation | async-start | bytes 8388608 | tf_op jit(solution)/shard_map/while
  400.0 5.3 slice-start.2
  412.8 7.8 %slice-start = ((s8[4718592]{0:T(1024)(128)(4,1)}), s8[4194304]{0:T(1024)(128)(4,1)S(1)}, s32[]{:S(2)}) async-start(s8[4718592]{0:T(1024)(128)(4,1)} %bitcast.22), calls=%async_computation | async-start | bytes 8388608 | tf_op jit(solution)/shard_map/while
  417.0 5.3 slice-start.2
  429.8 7.8 %slice-start = ((s8[4718592]{0:T(1024)(128)(4,1)}), s8[4194304]{0:T(1024)(128)(4,1)S(1)}, s32[]{:S(2)}) async-start(s8[4718592]{0:T(1024)(128)(4,1)} %bitcast.22), calls=%async_computation | async-start | bytes 8388608 | tf_op jit(solution)/shard_map/while
  434.0 5.3 slice-start.2
  446.8 7.8 %slice-start = ((s8[4718592]{0:T(1024)(128)(4,1)}), s8[4194304]{0:T(1024)(128)(4,1)S(1)}, s32[]{:S(2)}) async-start(s8[4718592]{0:T(1024)(128)(4,1)} %bitcast.22), calls=%async_computation | async-start | bytes 8388608 | tf_op jit(solution)/shard_map/while
  451.0 5.3 slice-start.2
  463.8 7.7 %slice-start = ((s8[4718592]{0:T(1024)(128)(4,1)}), s8[4194304]{0:T(1024)(128)(4,1)S(1)}, s32[]{:S(2)}) async-start(s8[4718592]{0:T(1024)(128)(4,1)} %bitcast.22), calls=%async_computation | async-start | bytes 8388608 | tf_op jit(solution)/shard_map/while
  467.8 5.3 slice-start.2
  477.4 3.8 copy-start.3
  482.5 101.5 %collective-permute-start.4 = (f32[6,24,16,256]{3,2,1,0:T(8,128)S(1)}, f32[6,24,16,256]{3,2,1,0:T(8,128)S(1)}, u32[]{:S(2)}, u32[]{:S(2)}) collective-permute-start(f32[6,24,16,256]{3,2,1,0:T(8,128)S(1)} %get-tuple-element.263), channel_id=1, source_target_pairs={{0,4},{4,8},{8,12},{12,16},{16,20},{20,24},{24,28},{1,5},{5,9},{9,... | collective-permute-start | bytes 7077896 | tf_op jit(solution)/shard_map/ppermute | solution.py:26
  487.0 97.6 %collective-permute-start.5 = (f32[6,24,16,256]{3,2,1,0:T(8,128)S(1)}, f32[6,24,16,256]{3,2,1,0:T(8,128)S(1)}, u32[]{:S(2)}, u32[]{:S(2)}) collective-permute-start(f32[6,24,16,256]{3,2,1,0:T(8,128)S(1)} %get-tuple-element.262), channel_id=1, source_target_pairs={{4,0},{8,4},{12,8},{16,12},{20,16},{24,20},{28,24},{5,1},{9,5},{13... | collective-permute-start | bytes 7077896 | tf_op jit(solution)/shard_map/ppermute | solution.py:26
  584.6 3.8 copy-start.1
  (69 other events, 171.6 us)
where the time goes:
time: 598 us; the launch traced here: 588 us
  waiting for transfers between devices  217 us (36%)
  local copies, waits for them, and re-layouts  175 us (29%)
  other arithmetic  119 us (20%)
  loops' own time  46 us (8%)
  starting transfers between devices  18.1 us (3%)
  between operations  12.4 us (2%)
    ppermute x2, waiting for transfers between devices, with_halo(): lax.ppermute(lax.slice_in_dim(block, block.shape[dim] - width, None, axis...  122 us
    ppermute x2, waiting for transfers between devices, passed_along(): return lax.ppermute(block, axis, route)  94.2 us
    dynamic_slice x17, local copies, waits for them, and re-layouts, step(): lax.dynamic_slice_in_dim(receiver_wide, MAXLAG + offset_lag, cells_x, 1)  70.1 us
    dynamic_slice x17, other arithmetic, step(): lax.dynamic_slice_in_dim(receiver_wide, MAXLAG + offset_lag, cells_x, 1)  61.6 us
    while x204, local copies, waits for them, and re-layouts  53.9 us
    dynamic_update_slice x34, other arithmetic, place_add(): return lax.dynamic_update_slice_in_dim(totals, current + values, start, 1)  46.9 us
    another operation x1, loops' own time, local(): source_total, receiver_total = lax.fori_loop(0, NOFF, step, (zeros, zeros))  46 us
  transfers between devices with their start and end apart: 6, of which 4 were waited for; matrix products, arithmetic and copies ran while one was open for 1% of the time, Pallas kernels for 0%

commit v1 on v0

v1 whole, which is shorter than its diff:
```python
import functools

import jax
import jax.numpy as jnp
from jax import lax
from jax.experimental import pallas as pl
from jax.experimental.pallas import tpu as pltpu
from jax.sharding import PartitionSpec as P

SUB = 8
LANES = 128
RADIUS = 2
MESH = pl.DeviceIdType.MESH
SWAP, NEAR, FAR, REST_UP, REST_DOWN, FAR_UP, FAR_DOWN, OUT = range(8)
KINDS = OUT + 2


def smooth_rows(rows):
    for _ in range(2 * RADIUS):
        rows = [low + high for low, high in zip(rows[:-1], rows[1:])]
    return rows


def gather_kernel(pairs, source, receiver, own, sent):
    parity = lax.rem(lax.axis_index("gx"), 2)
    for field, ref in enumerate((source, receiver)):
        for out, side in ((own, parity), (sent, 1 - parity)):
            at = pl.ds(pl.multiple_of(side * LANES, LANES), LANES)
            out[0, field] = jnp.swapaxes(ref[0, :, :, at], 0, 1)


def gather(snap_pairs, source_snaps, receiver_snaps):
    _, cells_x, cells_y, depth = source_snaps.shape
    pair_count = snap_pairs.shape[0]
    block = (1, cells_x, cells_y, depth)
    shape = (2, cells_y, cells_x, LANES)
    out = pl.BlockSpec((1, *shape), lambda p, pairs: (p, 0, 0, 0, 0))
    return pl.pallas_call(
        gather_kernel,
        out_shape=[jax.ShapeDtypeStruct((pair_count, *shape), jnp.float32)] * 2,
        grid_spec=pltpu.PrefetchScalarGridSpec(
            num_scalar_prefetch=1,
            grid=(pair_count,),
            in_specs=[
                pl.BlockSpec(block, lambda p, pairs: (pairs[p, 0], 0, 0, 0)),
                pl.BlockSpec(block, lambda p, pairs: (pairs[p, 1], 0, 0, 0)),
            ],
            out_specs=[out, out],
        ),
        compiler_params=pltpu.CompilerParams(vmem_limit_bytes=16 * 1024 * 1024),
        name="gather",
    )(snap_pairs, source_snaps, receiver_snaps)


def adjoint_kernel(
    gx, gy, lags, weights, rows_of, own, sent, out_s, out_r, *scratch
):
    pair_count = own.shape[0]
    cells_y, cells_x = own.shape[2:4]
    wides = scratch[:pair_count]
    stages = scratch[pair_count : 2 * pair_count]
    send_sem, recv_sem, own_sem, mine_sem = scratch[2 * pair_count :]
    outs = (out_s, out_r)
    noff = lags.shape[0]
    blocks = cells_x // SUB

    ix = lax.axis_index("gx")
    iy = lax.axis_index("gy")
    parity = lax.rem(ix, 2)
    partner = ix + 1 - 2 * parity
    outward = ix - 2 + 4 * parity
    inward = ix + 2 - 4 * parity
    has_out = (outward >= 0) & (outward < gx)
    has_in = (inward >= 0) & (inward < gx)
    has_low = iy > 0
    has_high = iy < gy - 1

    own_at = pl.ds(pl.multiple_of(cells_x + cells_x * parity, SUB), cells_x)
    recv_at = pl.ds(pl.multiple_of(2 * cells_x - cells_x * parity, SUB), cells_x)
    near_at = pl.ds(pl.multiple_of(3 * cells_x - 3 * cells_x * parity, SUB), cells_x)
    far_at = pl.ds(pl.multiple_of(3 * cells_x * parity, SUB), cells_x)
    rest_at = pl.ds(pl.multiple_of(cells_x - cells_x * parity, SUB), 3 * cells_x)
    core = pl.ds(RADIUS, cells_y)
    lane_at = pl.ds(pl.multiple_of(parity * LANES, LANES), LANES)

    barrier = pltpu.get_barrier_semaphore()

    def greet(axis, index):
        pl.semaphore_signal(barrier, inc=1, device_id={axis: index}, device_id_type=MESH)

    greet("gx", partner)
    pl.when(has_out)(lambda: greet("gx", outward))
    pl.when(has_in)(lambda: greet("gx", inward))
    pl.when(has_low)(lambda: greet("gy", iy - 1))
    pl.when(has_high)(lambda: greet("gy", iy + 1))

    for wide in wides:
        for field in range(2):

            @pl.when(jnp.logical_not(has_in))
            def _():
                wide[field, core, near_at, :] = jnp.zeros((cells_y, cells_x, LANES), jnp.float32)

            @pl.when(jnp.logical_not(has_out))
            def _():
                wide[field, core, far_at, :] = jnp.zeros((cells_y, cells_x, LANES), jnp.float32)

            edge = jnp.zeros((RADIUS, 4 * cells_x, LANES), jnp.float32)

            @pl.when(jnp.logical_not(has_low))
            def _():
                wide[field, pl.ds(0, RADIUS)] = edge

            @pl.when(jnp.logical_not(has_high))
            def _():
                wide[field, pl.ds(cells_y + RADIUS, RADIUS)] = edge

    pl.semaphore_wait(
        barrier,
        1 + sum(flag.astype(jnp.int32) for flag in (has_out, has_in, has_low, has_high)),
    )

    def remote(pair, kind, src, dst, axis, index):
        return pltpu.make_async_remote_copy(
            src_ref=src,
            dst_ref=dst,
            send_sem=send_sem.at[pair, kind],
            recv_sem=recv_sem.at[pair, kind],
            device_id={axis: index},
            device_id_type=MESH,
        )

    def swap_copy(pair):
        dst = wides[pair].at[:, core, own_at, :]
        return remote(pair, SWAP, sent.at[pair], dst, "gx", partner)

    def swap_arrival(pair):
        dst = wides[pair].at[:, core, recv_at, :]
        return remote(pair, SWAP, sent.at[pair], dst, "gx", partner)

    def near_copy(pair):
        return remote(
            pair, NEAR, own.at[pair], wides[pair].at[:, core, near_at, :], "gx", outward
        )

    def far_copy(pair):
        wide = wides[pair]
        return remote(
            pair,
            FAR,
            wide.at[:, core, recv_at, :],
            wide.at[:, core, far_at, :],
            "gx",
            inward,
        )

    def edge_copies(pair, kind, at):
        wide = wides[pair]
        size = RADIUS
        up = remote(
            pair,
            kind,
            wide.at[:, pl.ds(cells_y, size), at, :],
            wide.at[:, pl.ds(0, size), at, :],
            "gy",
            iy + 1,
        )
        down = remote(
            pair,
            kind + 1,
            wide.at[:, pl.ds(RADIUS, size), at, :],
            wide.at[:, pl.ds(cells_y + RADIUS, size), at, :],
            "gy",
            iy - 1,
        )
        return up, down

    def start_edges(pair, kind, at):
        up, down = edge_copies(pair, kind, at)
        pl.when(has_high)(up.start)
        pl.when(has_low)(down.start)

    def wait_edges(pair, kind, at):
        up, down = edge_copies(pair, kind, at)
        pl.when(has_low)(up.wait_recv)
        pl.when(has_high)(down.wait_recv)

    def own_copy(pair):
        return pltpu.make_async_copy(
            own.at[pair], wides[pair].at[:, core, own_at, :], own_sem.at[pair]
        )

    def out_copy(pair, field):
        return remote(
            pair,
            OUT + field,
            stages[pair].at[1, field],
            outs[field].at[pair, :, lane_at],
            "gx",
            partner,
        )

    def out_arrival(pair, field):
        theirs = pl.ds(pl.multiple_of((1 - parity) * LANES, LANES), LANES)
        return remote(
            pair,
            OUT + field,
            stages[pair].at[1, field],
            outs[field].at[pair, :, theirs],
            "gx",
            partner,
        )

    def mine_copy(pair, field):
        return pltpu.make_async_copy(
            stages[pair].at[0, field],
            outs[field].at[pair, :, lane_at],
            mine_sem.at[pair, field],
        )

    def compute(pair, side):
        wide, stage = wides[pair], stages[pair]
        rows = cells_y + 2 * RADIUS
        row = rows_of[pair]
        upper = side + parity - 2 * side * parity

        @pl.loop(0, 2 * blocks)
        def _(step):
            field = step // blocks
            block = step - field * blocks
            sign = 2 - 4 * field
            base = cells_x + upper * cells_x + block * SUB
            at = pl.ds(pl.multiple_of(base, SUB), SUB)
            centre = [wide[field, y, at, :] for y in range(rows)]

            def term(h, totals):
                moved = pl.ds(base + sign * lags[h], SUB)
                weight = weights[row, h] * 0.0625
                other = [wide[1 - field, y, moved, :] for y in range(rows)]
                image = smooth_rows([c * o for c, o in zip(centre, other)])
                return tuple(
                    total + (weight * value) * o
                    for total, value, o in zip(totals, image, other[RADIUS:])
                )

            zeros = tuple(jnp.zeros((SUB, LANES), jnp.float32) for _ in range(cells_y))
            totals = lax.fori_loop(0, noff, term, zeros)
            first = block * SUB * cells_y
            for y in range(cells_y):
                stage[side, field, pl.ds(first + y, SUB, stride=cells_y), :] = totals[y]

    pairs = range(pair_count)
    for pair in pairs:
        swap_copy(pair).start()
        pl.when(has_out)(near_copy(pair).start)
    for pair in pairs:
        own_copy(pair).start()
    for pair in pairs:
        own_copy(pair).wait()

    def forward(pair):
        swap_arrival(pair).wait_recv()
        pl.when(has_in)(far_copy(pair).start)
        pl.when(has_in)(near_copy(pair).wait_recv)
        start_edges(pair, REST_UP, rest_at)

    def finish(pair):
        pl.when(has_out)(far_copy(pair).wait_recv)
        start_edges(pair, FAR_UP, far_at)

    def settle(pair):
        wait_edges(pair, REST_UP, rest_at)
        wait_edges(pair, FAR_UP, far_at)

    forward(0)
    for pair in pairs:
        if pair + 1 < pair_count:
            forward(pair + 1)
        finish(pair)
        settle(pair)
        compute(pair, 1)
        for field in range(2):
            out_copy(pair, field).start()
        compute(pair, 0)
        for field in range(2):
            mine_copy(pair, field).start()

    for pair in pairs:
        swap_copy(pair).wait_send()
        pl.when(has_out)(near_copy(pair).wait_send)
        pl.when(has_in)(far_copy(pair).wait_send)
        for kind, at in ((REST_UP, rest_at), (FAR_UP, far_at)):
            up, down = edge_copies(pair, kind, at)
            pl.when(has_high)(up.wait_send)
            pl.when(has_low)(down.wait_send)
        for field in range(2):
            mine_copy(pair, field).wait()
            out_copy(pair, field).wait_send()
            out_arrival(pair, field).wait_recv()


def local(source_snaps, receiver_snaps, snap_pairs, offset_lags, weight_table, weight_index):
    _, cells_x, cells_y, depth = source_snaps.shape
    pair_count = snap_pairs.shape[0]
    own, sent = gather(snap_pairs, source_snaps, receiver_snaps)
    smem = pl.BlockSpec(memory_space=pltpu.SMEM)
    vmem = pl.BlockSpec(memory_space=pltpu.VMEM)
    anywhere = pl.BlockSpec(memory_space=pl.ANY)
    wide = pltpu.VMEM((2, cells_y + 2 * RADIUS, 4 * cells_x, LANES), jnp.float32)
    stage = pltpu.VMEM((2, 2, cells_x * cells_y, LANES), jnp.float32)
    out = pl.pallas_call(
        functools.partial(adjoint_kernel, lax.axis_size("gx"), lax.axis_size("gy")),
        out_shape=[
            jax.ShapeDtypeStruct((pair_count, cells_x * cells_y, depth), jnp.float32)
        ] * 2,
        in_specs=[smem] * 3 + [vmem] * 2,
        out_specs=[anywhere] * 2,
        scratch_shapes=[wide] * pair_count
        + [stage] * pair_count
        + [
            pltpu.SemaphoreType.DMA((pair_count, KINDS)),
            pltpu.SemaphoreType.DMA((pair_count, KINDS)),
            pltpu.SemaphoreType.DMA((pair_count,)),
            pltpu.SemaphoreType.DMA((pair_count, 2)),
        ],
        compiler_params=pltpu.CompilerParams(
            collective_id=0, has_side_effects=True, vmem_limit_bytes=48 * 1024 * 1024
        ),
        name="adjoints",
    )(offset_lags, weight_table, weight_index, own, sent)
    return tuple(a.reshape(pair_count, cells_x, cells_y, depth) for a in out)


def solution(mesh):
    return jax.shard_map(
        local,
        mesh=mesh,
        in_specs=(P(None, "gx", "gy", None), P(None, "gx", "gy", None), P(), P(), P(), P()),
        out_specs=(P(None, "gx", "gy", None), P(None, "gx", "gy", None)),
        check_vma=False,
    )
```

time: 598 us -> 127 us (0.21); the launches traced: 588 us -> 126 us
  waiting for transfers between devices: 217 us -> 0 us
  local copies, waits for them, and re-layouts: 175 us -> 10.2 us
  other arithmetic: 119 us -> 0 us
  Pallas kernels: 0 us -> 116 us
  loops' own time: 46 us -> 0 us
  starting transfers between devices: 18.1 us -> 0 us
  between operations: 12.4 us -> 0.66 us
    ppermute x6 -> x0, waiting for transfers between devices: 217 us -> none  [the longest x2 122 us: with_halo(): lax.ppermute(lax.slice_in_dim(block, block.shape[dim] - width, None, axis...]
    pallas_call x0 -> x2, Pallas kernels: none -> 116 us  [the longest x1 114 us: local(): pl.pallas_call(functools.partial(adjoint_kernel, lax.axis_size('gx'), lax...]
    dynamic_slice x36 -> x0, local copies, waits for them, and re-layouts: 82 us -> none  [the longest x17 70.1 us: step(): lax.dynamic_slice_in_dim(receiver_wide, MAXLAG + offset_lag, cells_x, 1)]
    dynamic_slice x17 -> x0, other arithmetic: 61.6 us -> none  [step(): lax.dynamic_slice_in_dim(receiver_wide, MAXLAG + offset_lag, cells_x, 1)]
    while x205 -> x0, local copies, waits for them, and re-layouts: 54.7 us -> none
    dynamic_update_slice x34 -> x0, other arithmetic: 46.9 us -> none  [place_add(): return lax.dynamic_update_slice_in_dim(totals, current + values, start, 1)]
    another operation x1 -> x0, loops' own time: 46 us -> none  [local(): source_total, receiver_total = lax.fori_loop(0, NOFF, step, (zeros, zeros))]
    slice x7 -> x0, local copies, waits for them, and re-layouts: 19.7 us -> none  [the longest x1 10.2 us: local(): receiver_wide = extended[pair_count:]]
  transfers between devices with their start and end apart: 6 -> 0, of which waited for: 4 -> 0; matrix products, arithmetic and copies ran while one was open for 1% -> 0% of each run, Pallas kernels for 0% -> 0%
where the time goes in v1:
time: 127 us; the launch traced here: 126 us
  Pallas kernels  116 us (91%)
  local copies, waits for them, and re-layouts  10.2 us (8%)
    pallas_call x1, Pallas kernels, local(): pl.pallas_call(functools.partial(adjoint_kernel, lax.axis_size('gx'), lax...  114 us
    unnamed x17, local copies, waits for them, and re-layouts  10.2 us

profile of v1, /device:TPU:6, one launch (start us, length us, event | category | flops | bytes accessed | tf_op | source)
XLA Modules:
  0.0 126.4 jit_solution(10154796310099574627)
XLA Ops:
  0.6 0.8 copy.8.pairs
  1.4 0.0 copy-start
  1.4 1.9 %copy-done = f32[4,48,16,256]{3,2,1,0:T(8,128)S(1)} copy-done((f32[4,48,16,256]{3,2,1,0:T(8,128)S(1)}, f32[4,48,16,256]{3,2,1,0:T(8,128)}, u32[]{:S(2)}) %copy-start) | copy-done | bytes 3145752
  3.3 0.0 copy-start.1
  3.3 1.9 %copy-done.1 = f32[4,48,16,256]{3,2,1,0:T(8,128)S(1)} copy-done((f32[4,48,16,256]{3,2,1,0:T(8,128)S(1)}, f32[4,48,16,256]{3,2,1,0:T(8,128)}, u32[]{:S(2)}) %copy-start.1) | copy-done | bytes 3145752
  5.2 0.0 copy-start.4
  5.2 0.0 copy-start.5
  5.2 0.0 copy-start.6
  5.2 1.6 %gather.1 = (f32[3,2,16,48,128]{4,3,2,1,0:T(8,128)S(1)}, f32[3,2,16,48,128]{4,3,2,1,0:T(8,128)S(1)}) custom-call(s32[3,2]{1,0:T(4,128)S(1)} %copy.8.pairs, f32[4,48,16,256]{3,2,1,0:T(8,128)S(1)} %copy-done, f32[4,48,16,256]{3,2,1,0:T(8,128)S(1)} %copy-done.1), custom_call_target="tpu_custom_call" | custom-call | tf_op jit(solution)/shard_map/gather/pallas_call | solution.py:38
  6.8 0.0 copy-start.2
  6.8 1.4 %copy-done.2 = f32[3,2,16,48,128]{4,3,2,1,0:T(8,128)} copy-done((f32[3,2,16,48,128]{4,3,2,1,0:T(8,128)}, f32[3,2,16,48,128]{4,3,2,1,0:T(8,128)S(1)}, u32[]{:S(2)}) %copy-start.2) | copy-done | bytes 2359320
  8.2 0.0 copy-start.3
  8.2 1.4 %copy-done.3 = f32[3,2,16,48,128]{4,3,2,1,0:T(8,128)} copy-done((f32[3,2,16,48,128]{4,3,2,1,0:T(8,128)}, f32[3,2,16,48,128]{4,3,2,1,0:T(8,128)S(1)}, u32[]{:S(2)}) %copy-start.3) | copy-done | bytes 2359320
  9.6 0.0 copy-done.4
  9.6 0.0 copy-done.5
  9.6 0.0 copy-done.6
  9.6 113.9 %adjoints.1 = (f32[3,768,256]{2,1,0:T(8,128)S(1)}, f32[3,768,256]{2,1,0:T(8,128)S(1)}) custom-call(s32[17]{0:T(128)S(1)} %copy-done.5, f32[4,17]{1,0:T(4,128)S(1)} %copy-done.4, s32[3]{0:T(128)S(1)} %copy-done.6, f32[3,2,16,48,128]{4,3,2,1,0:T(8,128)} %copy-done.2, f32[3,2,16,48,128]{4,3,2,1,0:T(8,128)} %copy-done.3), custom_call_target="tpu_custom_call" | custom-call | tf_op jit(solution)/shard_map/adjoints/pallas_call | solution.py:311
  123.6 1.4 %copy.11 = f32[3,48,16,256]{3,2,1,0:T(8,128)} copy(f32[3,48,16,256]{3,2,1,0:T(8,128)S(1)} %bitcast.3) | data formatting | bytes 4718592
  125.0 1.4 %copy.12 = f32[3,48,16,256]{3,2,1,0:T(8,128)} copy(f32[3,48,16,256]{3,2,1,0:T(8,128)S(1)} %bitcast.2) | data formatting | bytes 4718592
Async XLA Ops:
  1.4 1.9 %copy-start = (f32[4,48,16,256]{3,2,1,0:T(8,128)S(1)}, f32[4,48,16,256]{3,2,1,0:T(8,128)}, u32[]{:S(2)}) copy-start(f32[4,48,16,256]{3,2,1,0:T(8,128)} %source.1) | copy-start | bytes 9437188
  3.3 1.9 %copy-start.1 = (f32[4,48,16,256]{3,2,1,0:T(8,128)S(1)}, f32[4,48,16,256]{3,2,1,0:T(8,128)}, u32[]{:S(2)}) copy-start(f32[4,48,16,256]{3,2,1,0:T(8,128)} %receiver.1) | copy-start | bytes 9437188
  5.2 4.5 %copy-start.4 = (f32[4,17]{1,0:T(4,128)S(1)}, f32[4,17]{1,0:T(4,128)}, u32[]{:S(2)}) copy-start(f32[4,17]{1,0:T(4,128)} %weights.1) | copy-start | bytes 820
  5.2 4.5 %copy-start.5 = (s32[17]{0:T(128)S(1)}, s32[17]{0:T(128)}, u32[]{:S(2)}) copy-start(s32[17]{0:T(128)} %lags.1) | copy-start | bytes 208
  5.2 4.5 %copy-start.6 = (s32[3]{0:T(128)S(1)}, s32[3]{0:T(128)}, u32[]{:S(2)}) copy-start(s32[3]{0:T(128)} %rows_of.1) | copy-start | bytes 40
  6.8 1.4 %copy-start.2 = (f32[3,2,16,48,128]{4,3,2,1,0:T(8,128)}, f32[3,2,16,48,128]{4,3,2,1,0:T(8,128)S(1)}, u32[]{:S(2)}) copy-start(f32[3,2,16,48,128]{4,3,2,1,0:T(8,128)S(1)} %get-tuple-element.6.own) | copy-start | bytes 7077892
  8.2 1.4 %copy-start.3 = (f32[3,2,16,48,128]{4,3,2,1,0:T(8,128)}, f32[3,2,16,48,128]{4,3,2,1,0:T(8,128)S(1)}, u32[]{:S(2)}) copy-start(f32[3,2,16,48,128]{4,3,2,1,0:T(8,128)S(1)} %get-tuple-element.7.sent) | copy-start | bytes 7077892

commit v2 on v1

--- a/solution.py
+++ b/solution.py
@@ -47,7 +47,7 @@
             ],
             out_specs=[out, out],
         ),
-        compiler_params=pltpu.CompilerParams(vmem_limit_bytes=16 * 1024 * 1024),
+        compiler_params=pltpu.CompilerParams(vmem_limit_bytes=58 * 1024 * 1024),
         name="gather",
     )(snap_pairs, source_snaps, receiver_snaps)
 
@@ -304,7 +304,6 @@
     pair_count = snap_pairs.shape[0]
     own, sent = gather(snap_pairs, source_snaps, receiver_snaps)
     smem = pl.BlockSpec(memory_space=pltpu.SMEM)
-    vmem = pl.BlockSpec(memory_space=pltpu.VMEM)
     anywhere = pl.BlockSpec(memory_space=pl.ANY)
     wide = pltpu.VMEM((2, cells_y + 2 * RADIUS, 4 * cells_x, LANES), jnp.float32)
     stage = pltpu.VMEM((2, 2, cells_x * cells_y, LANES), jnp.float32)
@@ -313,7 +312,7 @@
         out_shape=[
             jax.ShapeDtypeStruct((pair_count, cells_x * cells_y, depth), jnp.float32)
         ] * 2,
-        in_specs=[smem] * 3 + [vmem] * 2,
+        in_specs=[smem] * 3 + [pl.BlockSpec(memory_space=pltpu.HBM)] * 2,
         out_specs=[anywhere] * 2,
         scratch_shapes=[wide] * pair_count
         + [stage] * pair_count

time: 127 us -> 124 us (0.976)
  local copies, waits for them, and re-layouts: 10.2 us -> 4.16 us
  Pallas kernels: 116 us -> 119 us
    unnamed x17 -> x9, local copies, waits for them, and re-layouts: 10.2 us -> 4.16 us
    pallas_call x1, Pallas kernels: 1.63 us -> 6.4 us  [gather(): pl.pallas_call(gather_kernel, out_shape=[jax.ShapeDtypeStruct((pair_count...]
    pallas_call x1, Pallas kernels: 114 us -> 112 us  [local(): pl.pallas_call(functools.partial(adjoint_kernel, lax.axis_size('gx'), lax...]
where the time goes in v2:
time: 124 us; the launch traced here: 123 us
  Pallas kernels  119 us (96%)
  local copies, waits for them, and re-layouts  4.16 us (3%)
    pallas_call x1, Pallas kernels, local(): pl.pallas_call(functools.partial(adjoint_kernel, lax.axis_size('gx'), lax...  112 us
    pallas_call x1, Pallas kernels, gather(): pl.pallas_call(gather_kernel, out_shape=[jax.ShapeDtypeStruct((pair_count...  6.4 us
    unnamed x9, local copies, waits for them, and re-layouts  4.16 us

profile of v2, /device:TPU:6, one launch (start us, length us, event | category | flops | bytes accessed | tf_op | source)
XLA Modules:
  0.0 123.5 jit_solution(5730101388002982049)
XLA Ops:
  0.6 1.3 %copy.8.pairs = s32[3,2]{1,0:T(4,128)} copy(s32[3,2]{0,1:T(2,128)} %param.8) | data formatting | bytes 48 | tf_op args[2]
  2.0 0.0 copy-start
  2.0 0.0 copy-start.1
  2.0 0.0 copy-start.2
  2.0 6.4 %gather.1 = (f32[3,2,16,48,128]{4,3,2,1,0:T(8,128)}, f32[3,2,16,48,128]{4,3,2,1,0:T(8,128)}) custom-call(s32[3,2]{1,0:T(4,128)} %copy.8.pairs, f32[4,48,16,256]{3,2,1,0:T(8,128)} %source.1, f32[4,48,16,256]{3,2,1,0:T(8,128)} %receiver.1), custom_call_target="tpu_custom_call" | custom-call | tf_op jit(solution)/shard_map/gather/pallas_call | solution.py:38
  8.4 0.0 copy-done
  8.4 0.0 copy-done.1
  8.4 0.0 copy-done.2
  8.4 112.3 %adjoints.1 = (f32[3,768,256]{2,1,0:T(8,128)S(1)}, f32[3,768,256]{2,1,0:T(8,128)S(1)}) custom-call(s32[17]{0:T(128)S(1)} %copy-done.1, f32[4,17]{1,0:T(4,128)S(1)} %copy-done, s32[3]{0:T(128)S(1)} %copy-done.2, f32[3,2,16,48,128]{4,3,2,1,0:T(8,128)} %get-tuple-element.6.own, f32[3,2,16,48,128]{4,3,2,1,0:T(8,128)} %get-tuple-element.7.sent), custom_call_target="tpu_custom_call" | custom-call | tf_op jit(solution)/shard_map/adjoints/pallas_call | solution.py:310
  120.7 1.4 %copy.11 = f32[3,48,16,256]{3,2,1,0:T(8,128)} copy(f32[3,48,16,256]{3,2,1,0:T(8,128)S(1)} %bitcast.3) | data formatting | bytes 4718592
  122.1 1.4 %copy.12 = f32[3,48,16,256]{3,2,1,0:T(8,128)} copy(f32[3,48,16,256]{3,2,1,0:T(8,128)S(1)} %bitcast.2) | data formatting | bytes 4718592
Async XLA Ops:
  2.0 6.4 %copy-start = (f32[4,17]{1,0:T(4,128)S(1)}, f32[4,17]{1,0:T(4,128)}, u32[]{:S(2)}) copy-start(f32[4,17]{1,0:T(4,128)} %weights.1) | copy-start | bytes 820
  2.0 6.4 %copy-start.1 = (s32[17]{0:T(128)S(1)}, s32[17]{0:T(128)}, u32[]{:S(2)}) copy-start(s32[17]{0:T(128)} %lags.1) | copy-start | bytes 208
  2.0 6.4 %copy-start.2 = (s32[3]{0:T(128)S(1)}, s32[3]{0:T(128)}, u32[]{:S(2)}) copy-start(s32[3]{0:T(128)} %rows_of.1) | copy-start | bytes 40

commit v3 on v2

--- a/solution.py
+++ b/solution.py
@@ -32,24 +32,24 @@
 def gather(snap_pairs, source_snaps, receiver_snaps):
     _, cells_x, cells_y, depth = source_snaps.shape
     pair_count = snap_pairs.shape[0]
-    block = (1, cells_x, cells_y, depth)
+    block = (1, cells_x, SUB, depth)
     shape = (2, cells_y, cells_x, LANES)
-    out = pl.BlockSpec((1, *shape), lambda p, pairs: (p, 0, 0, 0, 0))
+    out = pl.BlockSpec((1, 2, SUB, cells_x, LANES), lambda p, y, pairs: (p, 0, y, 0, 0))
     return pl.pallas_call(
         gather_kernel,
         out_shape=[jax.ShapeDtypeStruct((pair_count, *shape), jnp.float32)] * 2,
         grid_spec=pltpu.PrefetchScalarGridSpec(
             num_scalar_prefetch=1,
-            grid=(pair_count,),
+            grid=(pair_count, cells_y // SUB),
             in_specs=[
-                pl.BlockSpec(block, lambda p, pairs: (pairs[p, 0], 0, 0, 0)),
-                pl.BlockSpec(block, lambda p, pairs: (pairs[p, 1], 0, 0, 0)),
+                pl.BlockSpec(block, lambda p, y, pairs: (pairs[0, p], 0, y, 0)),
+                pl.BlockSpec(block, lambda p, y, pairs: (pairs[1, p], 0, y, 0)),
             ],
             out_specs=[out, out],
         ),
         compiler_params=pltpu.CompilerParams(vmem_limit_bytes=58 * 1024 * 1024),
         name="gather",
-    )(snap_pairs, source_snaps, receiver_snaps)
+    )(snap_pairs.T, source_snaps, receiver_snaps)
 
 
 def adjoint_kernel(
@@ -218,17 +218,16 @@
             mine_sem.at[pair, field],
         )
 
-    def compute(pair, side):
+    def compute(pair, side, field):
         wide, stage = wides[pair], stages[pair]
         rows = cells_y + 2 * RADIUS
         row = rows_of[pair]
         upper = side + parity - 2 * side * parity
 
-        @pl.loop(0, 2 * blocks)
-        def _(step):
-            field = step // blocks
-            block = step - field * blocks
-            sign = 2 - 4 * field
+        sign = 2 - 4 * field
+
+        @pl.loop(0, blocks)
+        def _(block):
             base = cells_x + upper * cells_x + block * SUB
             at = pl.ds(pl.multiple_of(base, SUB), SUB)
             centre = [wide[field, y, at, :] for y in range(rows)]
@@ -278,11 +277,11 @@
             forward(pair + 1)
         finish(pair)
         settle(pair)
-        compute(pair, 1)
         for field in range(2):
+            compute(pair, 1, field)
             out_copy(pair, field).start()
-        compute(pair, 0)
         for field in range(2):
+            compute(pair, 0, field)
             mine_copy(pair, field).start()
 
     for pair in pairs:

time: 124 us -> 119 us (0.960)
  Pallas kernels: 119 us -> 115 us
  local copies, waits for them, and re-layouts: 4.16 us -> 2.83 us
    pallas_call x1, Pallas kernels: 112 us -> 108 us  [local(): pl.pallas_call(functools.partial(adjoint_kernel, lax.axis_size('gx'), lax...]
    unnamed x9 -> x8, local copies, waits for them, and re-layouts: 4.16 us -> 2.83 us
where the time goes in v3:
time: 119 us; the launch traced here: 118 us
  Pallas kernels  115 us (97%)
  local copies, waits for them, and re-layouts  2.83 us (2%)
    pallas_call x1, Pallas kernels, local(): pl.pallas_call(functools.partial(adjoint_kernel, lax.axis_size('gx'), lax...  108 us
    pallas_call x1, Pallas kernels, gather(): pl.pallas_call(gather_kernel, out_shape=[jax.ShapeDtypeStruct((pair_count...  7.05 us
    unnamed x8, local copies, waits for them, and re-layouts  2.83 us

profile of v3, /device:TPU:6, one launch (start us, length us, event | category | flops | bytes accessed | tf_op | source)
XLA Modules:
  0.0 118.4 jit_solution(18054483559812481507)
XLA Ops:
  0.6 0.0 copy-start
  0.6 0.0 copy-start.1
  0.7 0.0 copy-start.2
  0.7 7.1 %gather.1 = (f32[3,2,16,48,128]{4,3,2,1,0:T(8,128)}, f32[3,2,16,48,128]{4,3,2,1,0:T(8,128)}) custom-call(s32[2,3]{1,0:T(2,128)} %bitcast.5, f32[4,48,16,256]{3,2,1,0:T(8,128)} %source.1, f32[4,48,16,256]{3,2,1,0:T(8,128)} %receiver.1), custom_call_target="tpu_custom_call" | custom-call | tf_op jit(solution)/shard_map/gather/pallas_call | solution.py:38
  7.7 0.0 copy-done
  7.7 0.0 copy-done.1
  7.7 0.0 copy-done.2
  7.7 107.8 %adjoints.1 = (f32[3,768,256]{2,1,0:T(8,128)S(1)}, f32[3,768,256]{2,1,0:T(8,128)S(1)}) custom-call(s32[17]{0:T(128)S(1)} %copy-done.1, f32[4,17]{1,0:T(4,128)S(1)} %copy-done, s32[3]{0:T(128)S(1)} %copy-done.2, f32[3,2,16,48,128]{4,3,2,1,0:T(8,128)} %get-tuple-element.6.own, f32[3,2,16,48,128]{4,3,2,1,0:T(8,128)} %get-tuple-element.7.sent), custom_call_target="tpu_custom_call" | custom-call | tf_op jit(solution)/shard_map/adjoints/pallas_call | solution.py:309
  115.6 1.4 %copy.10 = f32[3,48,16,256]{3,2,1,0:T(8,128)} copy(f32[3,48,16,256]{3,2,1,0:T(8,128)S(1)} %bitcast.4) | data formatting | bytes 4718592
  117.0 1.4 %copy.11 = f32[3,48,16,256]{3,2,1,0:T(8,128)} copy(f32[3,48,16,256]{3,2,1,0:T(8,128)S(1)} %bitcast.3) | data formatting | bytes 4718592
Async XLA Ops:
  0.6 7.1 %copy-start = (f32[4,17]{1,0:T(4,128)S(1)}, f32[4,17]{1,0:T(4,128)}, u32[]{:S(2)}) copy-start(f32[4,17]{1,0:T(4,128)} %weights.1) | copy-start | bytes 820
  0.6 7.1 %copy-start.1 = (s32[17]{0:T(128)S(1)}, s32[17]{0:T(128)}, u32[]{:S(2)}) copy-start(s32[17]{0:T(128)} %lags.1) | copy-start | bytes 208
  0.7 7.1 %copy-start.2 = (s32[3]{0:T(128)S(1)}, s32[3]{0:T(128)}, u32[]{:S(2)}) copy-start(s32[3]{0:T(128)} %rows_of.1) | copy-start | bytes 40

commit v4 on v3

--- a/solution.py
+++ b/solution.py
@@ -21,32 +21,54 @@
     return rows
 
 
-def gather_kernel(pairs, source, receiver, own, sent):
+def gather_kernel(pairs, source, receiver, own, sent, held, turned, in_sem, out_sem):
     parity = lax.rem(lax.axis_index("gx"), 2)
-    for field, ref in enumerate((source, receiver)):
-        for out, side in ((own, parity), (sent, 1 - parity)):
-            at = pl.ds(pl.multiple_of(side * LANES, LANES), LANES)
-            out[0, field] = jnp.swapaxes(ref[0, :, :, at], 0, 1)
+    pair_count = own.shape[0]
+
+    def read(pair, field):
+        ref = (source, receiver)[field]
+        return pltpu.make_async_copy(
+            ref.at[pairs[field, pair]], held.at[pair, field], in_sem.at[pair, field]
+        )
+
+    def write(pair, which):
+        out = (own, sent)[which]
+        return pltpu.make_async_copy(
+            turned.at[pair, which], out.at[pair], out_sem.at[pair, which]
+        )
+
+    for pair in range(pair_count):
+        for field in range(2):
+            read(pair, field).start()
+    for pair in range(pair_count):
+        for field in range(2):
+            read(pair, field).wait()
+            for which, side in enumerate((parity, 1 - parity)):
+                at = pl.ds(pl.multiple_of(side * LANES, LANES), LANES)
+                turned[pair, which, field] = jnp.swapaxes(held[pair, field, :, :, at], 0, 1)
+        for which in range(2):
+            write(pair, which).start()
+    for pair in range(pair_count):
+        for which in range(2):
+            write(pair, which).wait()
 
 
 def gather(snap_pairs, source_snaps, receiver_snaps):
     _, cells_x, cells_y, depth = source_snaps.shape
     pair_count = snap_pairs.shape[0]
-    block = (1, cells_x, SUB, depth)
     shape = (2, cells_y, cells_x, LANES)
-    out = pl.BlockSpec((1, 2, SUB, cells_x, LANES), lambda p, y, pairs: (p, 0, y, 0, 0))
+    anywhere = pl.BlockSpec(memory_space=pl.ANY)
     return pl.pallas_call(
         gather_kernel,
         out_shape=[jax.ShapeDtypeStruct((pair_count, *shape), jnp.float32)] * 2,
-        grid_spec=pltpu.PrefetchScalarGridSpec(
-            num_scalar_prefetch=1,
-            grid=(pair_count, cells_y // SUB),
-            in_specs=[
-                pl.BlockSpec(block, lambda p, y, pairs: (pairs[0, p], 0, y, 0)),
-                pl.BlockSpec(block, lambda p, y, pairs: (pairs[1, p], 0, y, 0)),
-            ],
-            out_specs=[out, out],
-        ),
+        in_specs=[pl.BlockSpec(memory_space=pltpu.SMEM), anywhere, anywhere],
+        out_specs=[anywhere, anywhere],
+        scratch_shapes=[
+            pltpu.VMEM((pair_count, 2, cells_x, cells_y, depth), jnp.float32),
+            pltpu.VMEM((pair_count, 2, *shape), jnp.float32),
+            pltpu.SemaphoreType.DMA((pair_count, 2)),
+            pltpu.SemaphoreType.DMA((pair_count, 2)),
+        ],
         compiler_params=pltpu.CompilerParams(vmem_limit_bytes=58 * 1024 * 1024),
         name="gather",
     )(snap_pairs.T, source_snaps, receiver_snaps)

time: 119 us -> 117 us (0.983)
  Pallas kernels: 115 us -> 112 us
    pallas_call x1, Pallas kernels: 7.05 us -> 4.64 us  [gather(): pl.pallas_call(gather_kernel, out_shape=[jax.ShapeDtypeStruct((pair_count...]
where the time goes in v4:
time: 117 us; the launch traced here: 116 us
  Pallas kernels  112 us (96%)
  local copies, waits for them, and re-layouts  2.83 us (2%)
    pallas_call x1, Pallas kernels, local(): pl.pallas_call(functools.partial(adjoint_kernel, lax.axis_size('gx'), lax...  108 us
    pallas_call x1, Pallas kernels, gather(): pl.pallas_call(gather_kernel, out_shape=[jax.ShapeDtypeStruct((pair_count...  4.64 us
    unnamed x8, local copies, waits for them, and re-layouts  2.83 us

profile of v4, /device:TPU:6, one launch (start us, length us, event | category | flops | bytes accessed | tf_op | source)
XLA Modules:
  0.0 116.0 jit_solution(6064777963583311657)
XLA Ops:
  0.6 0.0 copy-start
  0.6 0.0 copy-start.1
  0.7 0.0 copy-start.2
  0.7 4.6 %gather.1 = (f32[3,2,16,48,128]{4,3,2,1,0:T(8,128)}, f32[3,2,16,48,128]{4,3,2,1,0:T(8,128)}) custom-call(s32[2,3]{1,0:T(2,128)} %bitcast.5, f32[4,48,16,256]{3,2,1,0:T(8,128)} %source.1, f32[4,48,16,256]{3,2,1,0:T(8,128)} %receiver.1), custom_call_target="tpu_custom_call" | custom-call | tf_op jit(solution)/shard_map/gather/pallas_call | solution.py:61
  5.3 0.0 copy-done
  5.3 0.0 copy-done.1
  5.3 0.0 copy-done.2
  5.3 107.8 %adjoints.1 = (f32[3,768,256]{2,1,0:T(8,128)S(1)}, f32[3,768,256]{2,1,0:T(8,128)S(1)}) custom-call(s32[17]{0:T(128)S(1)} %copy-done.1, f32[4,17]{1,0:T(4,128)S(1)} %copy-done, s32[3]{0:T(128)S(1)} %copy-done.2, f32[3,2,16,48,128]{4,3,2,1,0:T(8,128)} %get-tuple-element.6.own, f32[3,2,16,48,128]{4,3,2,1,0:T(8,128)} %get-tuple-element.7.sent), custom_call_target="tpu_custom_call" | custom-call | tf_op jit(solution)/shard_map/adjoints/pallas_call | solution.py:331
  113.2 1.4 %copy.10 = f32[3,48,16,256]{3,2,1,0:T(8,128)} copy(f32[3,48,16,256]{3,2,1,0:T(8,128)S(1)} %bitcast.4) | data formatting | bytes 4718592
  114.6 1.4 %copy.11 = f32[3,48,16,256]{3,2,1,0:T(8,128)} copy(f32[3,48,16,256]{3,2,1,0:T(8,128)S(1)} %bitcast.3) | data formatting | bytes 4718592
Async XLA Ops:
  0.6 4.7 %copy-start = (f32[4,17]{1,0:T(4,128)S(1)}, f32[4,17]{1,0:T(4,128)}, u32[]{:S(2)}) copy-start(f32[4,17]{1,0:T(4,128)} %weights.1) | copy-start | bytes 820
  0.6 4.7 %copy-start.1 = (s32[17]{0:T(128)S(1)}, s32[17]{0:T(128)}, u32[]{:S(2)}) copy-start(s32[17]{0:T(128)} %lags.1) | copy-start | bytes 208
  0.7 4.7 %copy-start.2 = (s32[3]{0:T(128)S(1)}, s32[3]{0:T(128)}, u32[]{:S(2)}) copy-start(s32[3]{0:T(128)} %rows_of.1) | copy-start | bytes 40

commit v5 on v4

--- a/solution.py
+++ b/solution.py
@@ -31,10 +31,10 @@
             ref.at[pairs[field, pair]], held.at[pair, field], in_sem.at[pair, field]
         )
 
-    def write(pair, which):
+    def write(pair, which, field):
         out = (own, sent)[which]
         return pltpu.make_async_copy(
-            turned.at[pair, which], out.at[pair], out_sem.at[pair, which]
+            turned.at[pair, which, field], out.at[pair, field], out_sem.at[pair, which, field]
         )
 
     for pair in range(pair_count):
@@ -46,11 +46,11 @@
             for which, side in enumerate((parity, 1 - parity)):
                 at = pl.ds(pl.multiple_of(side * LANES, LANES), LANES)
                 turned[pair, which, field] = jnp.swapaxes(held[pair, field, :, :, at], 0, 1)
-        for which in range(2):
-            write(pair, which).start()
+                write(pair, which, field).start()
     for pair in range(pair_count):
-        for which in range(2):
-            write(pair, which).wait()
+        for field in range(2):
+            for which in range(2):
+                write(pair, which, field).wait()
 
 
 def gather(snap_pairs, source_snaps, receiver_snaps):
@@ -67,7 +67,7 @@
             pltpu.VMEM((pair_count, 2, cells_x, cells_y, depth), jnp.float32),
             pltpu.VMEM((pair_count, 2, *shape), jnp.float32),
             pltpu.SemaphoreType.DMA((pair_count, 2)),
-            pltpu.SemaphoreType.DMA((pair_count, 2)),
+            pltpu.SemaphoreType.DMA((pair_count, 2, 2)),
         ],
         compiler_params=pltpu.CompilerParams(vmem_limit_bytes=58 * 1024 * 1024),
         name="gather",

time: 117 us -> 117 us (level)
  no operation moved by 1% of the time
where the time goes in v5:
time: 117 us; the launch traced here: 116 us
  Pallas kernels  113 us (97%)
  local copies, waits for them, and re-layouts  2.83 us (2%)
    pallas_call x1, Pallas kernels, local(): pl.pallas_call(functools.partial(adjoint_kernel, lax.axis_size('gx'), lax...  108 us
    pallas_call x1, Pallas kernels, gather(): pl.pallas_call(gather_kernel, out_shape=[jax.ShapeDtypeStruct((pair_count...  4.71 us
    unnamed x8, local copies, waits for them, and re-layouts  2.83 us

profile of v5, /device:TPU:6, one launch (start us, length us, event | category | flops | bytes accessed | tf_op | source)
XLA Modules:
  0.0 116.1 jit_solution(14363961420994385517)
XLA Ops:
  0.6 0.0 copy-start
  0.6 0.0 copy-start.1
  0.7 0.0 copy-start.2
  0.7 4.7 %gather.1 = (f32[3,2,16,48,128]{4,3,2,1,0:T(8,128)}, f32[3,2,16,48,128]{4,3,2,1,0:T(8,128)}) custom-call(s32[2,3]{1,0:T(2,128)} %bitcast.5, f32[4,48,16,256]{3,2,1,0:T(8,128)} %source.1, f32[4,48,16,256]{3,2,1,0:T(8,128)} %receiver.1), custom_call_target="tpu_custom_call" | custom-call | tf_op jit(solution)/shard_map/gather/pallas_call | solution.py:61
  5.4 0.0 copy-done
  5.4 0.0 copy-done.1
  5.4 0.0 copy-done.2
  5.4 107.8 %adjoints.1 = (f32[3,768,256]{2,1,0:T(8,128)S(1)}, f32[3,768,256]{2,1,0:T(8,128)S(1)}) custom-call(s32[17]{0:T(128)S(1)} %copy-done.1, f32[4,17]{1,0:T(4,128)S(1)} %copy-done, s32[3]{0:T(128)S(1)} %copy-done.2, f32[3,2,16,48,128]{4,3,2,1,0:T(8,128)} %get-tuple-element.6.own, f32[3,2,16,48,128]{4,3,2,1,0:T(8,128)} %get-tuple-element.7.sent), custom_call_target="tpu_custom_call" | custom-call | tf_op jit(solution)/shard_map/adjoints/pallas_call | solution.py:331
  113.3 1.4 %copy.10 = f32[3,48,16,256]{3,2,1,0:T(8,128)} copy(f32[3,48,16,256]{3,2,1,0:T(8,128)S(1)} %bitcast.4) | data formatting | bytes 4718592
  114.7 1.4 %copy.11 = f32[3,48,16,256]{3,2,1,0:T(8,128)} copy(f32[3,48,16,256]{3,2,1,0:T(8,128)S(1)} %bitcast.3) | data formatting | bytes 4718592
Async XLA Ops:
  0.6 4.8 %copy-start = (f32[4,17]{1,0:T(4,128)S(1)}, f32[4,17]{1,0:T(4,128)}, u32[]{:S(2)}) copy-start(f32[4,17]{1,0:T(4,128)} %weights.1) | copy-start | bytes 820
  0.6 4.8 %copy-start.1 = (s32[17]{0:T(128)S(1)}, s32[17]{0:T(128)}, u32[]{:S(2)}) copy-start(s32[17]{0:T(128)} %lags.1) | copy-start | bytes 208
  0.7 4.8 %copy-start.2 = (s32[3]{0:T(128)S(1)}, s32[3]{0:T(128)}, u32[]{:S(2)}) copy-start(s32[3]{0:T(128)} %rows_of.1) | copy-start | bytes 40
